TPU v7x, 256 devices: a whole 4x4x8 slice. The times are simulated.
256 devices in a mesh: nodes: 32 (over y, x, core), queries: 8 (over z).
Axes of the slice: x: 4, y: 4, z: 8, core: 2. Of those that a mesh axis runs over, the one named last changes fastest.
Arguments:
- state_in: float32 [8192, 1024], P('nodes', 'queries')
- edge_src: int32 [131072], P('nodes'), may hold values from 0 to 2303
- edge_dst: int32 [131072], P('nodes'), may hold values from 0 to 255
- edge_rel: int32 [131072], P('nodes'), may hold values from 0 to 534
- edge_count: int32 [32], P('nodes'), may hold values from 1024 to 4096, as said below
- send_list: int32 [32, 32, 64], P('nodes'), may hold values from 0 to 255
- query_head: int32 [32], P('queries'), may hold values from 0 to 8191
- query_rel: int32 [32], P('queries'), may hold values from 0 to 534
- pos_tail: int32 [32], P('queries'), may hold values from 0 to 8191
- neg_ids: int32 [32, 4096], P('queries', 'nodes'), may hold values from 0 to 255
- rel_table: float32 [535, 32], replicated, may hold values from -1.8 to 1.8
- layer_weight: float32 [32, 32], replicated, may hold values from -1 to 1
- mlp_entity: float32 [32, 64], replicated, may hold values from -1 to 1
- mlp_query: float32 [32, 64], replicated, may hold values from -1 to 1
- score_weight: float32 [64], replicated, may hold values from -0.75 to 0.75
Outputs:
- new_state: float32 [8192, 1024], P('nodes', 'queries')
- loss: float32 [32], P('queries')
- grad_rel: float32 [535, 32], replicated
- grad_layer: float32 [32, 32], replicated
- grad_entity: float32 [32, 64], replicated
- grad_query: float32 [32, 64], replicated
- grad_score: float32 [64], replicated
Inputs may be any that keep to these rules, and one draw needn't show every extreme that they name: `edge_count`: some partition holds exactly 4096 live edges.
All inputs are finite; a program needn't handle non-finite values.
Results may differ from a plain program's by a relative error of at most 0.0003.
Values sent between devices are 32-bit elements; how exact they have to be, the bound alone decides.
A program may use at most 64 MiB of HBM per device.

v0:
```python
import functools

import jax
import jax.numpy as jnp
from jax import lax
from jax.experimental import pallas as pl
from jax.experimental.pallas import tpu as pltpu
from jax.sharding import PartitionSpec as P

adversarial = 0.5
MESH = pl.DeviceIdType.MESH
HIGH = lax.Precision.HIGHEST
F32 = jnp.float32
BF16 = jnp.bfloat16
NT = (((1,), (1,)), ((), ()))
NN = (((1,), (0,)), ((), ()))
TILES = 24
RELP = 640
BLK = 256


def mm(a, b, dims=NN, precision=None):
    return lax.dot_general(a, b, dims, precision=precision, preferred_element_type=F32)


def split(x, terms):
    parts = []
    for i in range(terms):
        part = x.astype(BF16)
        parts.append(part)
        if i + 1 < terms:
            x = x - part.astype(F32)
    return jnp.concatenate(parts, axis=0)


def join(y, terms):
    rows = y.shape[0] // terms
    out = y[:rows]
    for i in range(1, terms):
        out = out + y[i * rows : (i + 1) * rows]
    return out


def onehot(row, depth, base=0):
    ids = lax.broadcasted_iota(jnp.int32, (depth, row.shape[1]), 0)
    return jnp.where(ids == row - base, 1.0, 0.0).astype(BF16)


def lanes_of(x, queries, rows):
    return jnp.concatenate([x[q * rows : (q + 1) * rows] for q in range(queries)], axis=1)


def softplus(x):
    return jnp.maximum(x, 0.0) + jnp.log1p(jnp.exp(-jnp.abs(x)))


def sigmoid(x):
    return 1.0 / (1.0 + jnp.exp(-x))


def kernel(
    cfg,
    state, esrc, edst, erel, slist, neg, rel, wl, me_w, mq_w, sw, ecount, qhead, qrel, ptail,
    new_out, loss_out, grel_out, glayer_out, gent_out, gquery_out, gscore_out,
    st3, slrow, relpad, rt3, sbuf, recv, ort, odt, relg, acc, msg3, et2, onr,
    tsend, trecv, gmat, rsrc, rsbuf, zbuf, agbuf,
    s_send, s_recv, t_send, t_recv, r_send, r_recv, z_send, z_recv, a_send, a_recv,
):
    nodes, zs, nx, ny, queries_total = cfg
    me = lax.axis_index("nodes")
    mz = lax.axis_index("queries")
    chip = me // 2
    core = me % 2
    cx = chip % nx
    cy = chip // nx
    chips = nx * ny
    dd = wl.shape[0]
    hid = me_w.shape[1]
    ent = state.shape[0]
    nq = state.shape[1] // dd
    edges = esrc.shape[0] * 128
    blocks = edges // BLK
    negs = neg.shape[1]
    nrel = rel.shape[0]
    lane128 = lax.broadcasted_iota(jnp.int32, (1, 128), 1)
    low = lane128 < 64

    def node_of(t):
        return (t, mz)

    barrier = pltpu.get_barrier_semaphore()

    @pl.loop(1, nodes)
    def _(k):
        pl.semaphore_signal(barrier, inc=1, device_id=node_of((me + k) % nodes), device_id_type=MESH)

    @pl.loop(1, zs)
    def _(k):
        pl.semaphore_signal(barrier, inc=1, device_id=(me, (mz + k) % zs), device_id_type=MESH)

    stt = jnp.concatenate([state[i * 128 : (i + 1) * 128, :].T for i in range(ent // 128)], axis=1)
    st3[...] = split(stt, 3)
    slrow[:, 0:64] = slist[...]
    slrow[:, 64:128] = slist[...]

    pl.semaphore_wait(barrier, nodes - 1 + zs - 1)

    def chip_at(s, sign):
        tx = (cx + sign * (s % nx) + nx) % nx
        ty = (cy + sign * (s // nx) + ny) % ny
        return ty * nx + tx

    @pl.loop(0, chips)
    def _(s):
        tc = chip_at(s, 1)
        row = jnp.where(low, slrow[pl.ds(2 * tc, 1), :], slrow[pl.ds(2 * tc + 1, 1), :])
        got = join(mm(st3[...], onehot(row, ent)), 3)
        top, bot = got[:64], got[64:]
        c0 = jnp.where(low, top, pltpu.roll(bot, 64, 1))
        c1 = jnp.where(low, pltpu.roll(top, 64, 1), bot)
        sbuf[2 * s] = c0
        sbuf[2 * s + 1] = c1
        for c in range(2):
            @pl.when((s > 0) | (core != c))
            def _():
                pltpu.make_async_remote_copy(
                    src_ref=sbuf.at[2 * s + c],
                    dst_ref=recv.at[2 * s + core],
                    send_sem=s_send.at[2 * s + c],
                    recv_sem=s_recv.at[2 * s + core],
                    device_id=node_of(2 * tc + c),
                    device_id_type=MESH,
                ).start()

    recv[core] = sbuf[core]

    relpad[...] = jnp.zeros_like(relpad)
    relpad[0:nrel, 0:dd] = rel[...]
    relt = jnp.concatenate([relpad[i * 128 : (i + 1) * 128, :].T[:dd] for i in range(RELP // 128)], axis=1)
    rt3[...] = split(relt, 3)

    def edge_row(ref, j):
        return jnp.concatenate([ref[pl.ds(2 * j, 1), :], ref[pl.ds(2 * j + 1, 1), :]], axis=1)

    def cols(j):
        return pl.ds(pl.multiple_of(j * BLK, BLK), BLK)

    lane256 = lax.broadcasted_iota(jnp.int32, (1, BLK), 1)

    @pl.loop(0, blocks)
    def _(j):
        hot = onehot(edge_row(erel, j), RELP)
        ort[:, cols(j)] = hot
        relg[:, cols(j)] = join(mm(rt3[...], hot), 3)
        dst = jnp.where(lane256 + j * BLK < ecount[0], edge_row(edst, j), -1)
        odt[:, cols(j)] = onehot(dst, ent)
        acc[:, cols(j)] = join(mm(st3[...], onehot(edge_row(esrc, j), ent)), 3)

    @pl.loop(0, chips // 2)
    def _(t):
        for k in range(4):
            slot = 4 * t + k

            @pl.when((t > 0) | (k != core))
            def _():
                pltpu.make_async_copy(recv.at[slot], recv.at[slot], s_recv.at[slot]).wait()

        def pair(i):
            a, b = recv[4 * t + 2 * i], recv[4 * t + 2 * i + 1]
            top = jnp.where(low, a, pltpu.roll(b, 64, 1))
            bot = jnp.where(low, pltpu.roll(a, 64, 1), b)
            return jnp.concatenate([top, bot], axis=0)

        part = split(jnp.concatenate([pair(0), pair(1)], axis=1), 3)
        base0 = ent + 128 * chip_at(2 * t, -1)
        base1 = ent + 128 * chip_at(2 * t + 1, -1)

        @pl.loop(0, blocks)
        def _(j):
            row = edge_row(esrc, j)
            hot = jnp.concatenate([onehot(row, 128, base0), onehot(row, 128, base1)], axis=0)
            acc[:, cols(j)] += join(mm(part, hot), 3)

    @pl.loop(0, blocks)
    def _(j):
        r = relg[:, cols(j)]
        msg3[:, cols(j)] = split(acc[:, cols(j)] * jnp.concatenate([r] * nq, axis=0), 3)

    summed = join(mm(msg3[...], odt[...], NT), 3)

    def scalar_lanes(ref):
        out = jnp.full((1, 128), -1, jnp.int32)
        for q in range(nq):
            out = jnp.where(lane128 == q, ref[q], out)
        return out

    relhot = onehot(scalar_lanes(qrel), RELP)
    qvt = join(mm(rt3[...], relhot), 3)
    lane_ent = lax.broadcasted_iota(jnp.int32, (1, ent), 1)

    def local_of(g):
        return jnp.where(g // ent == me, g % ent, -1)

    heads = [jnp.where(lane_ent == local_of(qhead[q]), 1.0, 0.0) for q in range(nq)]
    s_all = lanes_of(summed, nq, dd) + jnp.concatenate(
        [qvt[:, q : q + 1] * heads[q] for q in range(nq)], axis=1
    )
    stt = jnp.concatenate([state[i * 128 : (i + 1) * 128, :].T for i in range(ent // 128)], axis=1)
    pre = mm(wl[...].T, s_all, precision=HIGH)
    new_all = lanes_of(stt, nq, dd) + jnp.maximum(pre, 0.0)
    new_t = jnp.concatenate([new_all[:, q * ent : (q + 1) * ent] for q in range(nq)], axis=0)
    for i in range(ent // 128):
        new_out[i * 128 : (i + 1) * 128, :] = new_t[:, i * 128 : (i + 1) * 128].T

    rows = 2 * negs
    lane_row = lax.broadcasted_iota(jnp.int32, (1, rows), 1)
    picks = []
    pos_mask = []
    for q in range(nq):
        pos = local_of(ptail[q])
        pos_mask.append((lane_row == negs) & (pos >= 0))
        wide = jnp.concatenate([neg[q : q + 1, :], jnp.full((1, negs), 0, jnp.int32) + pos], axis=1)
        hot = onehot(jnp.where(lane_row <= negs, wide, -1), ent)
        onr[q] = hot
        picks.append(join(mm(split(new_t[q * dd : (q + 1) * dd], 3), hot), 3))
    picked = jnp.concatenate(picks, axis=1)
    is_neg = jnp.concatenate([lane_row < negs] * nq, axis=1)
    is_pos = jnp.concatenate(pos_mask, axis=1)
    qh = mm(mq_w[...].T, qvt, precision=HIGH)
    pre_h = mm(me_w[...].T, picked, precision=HIGH) + jnp.concatenate(
        [jnp.broadcast_to(qh[:, q : q + 1], (hid, rows)) for q in range(nq)], axis=1
    )
    act = jnp.maximum(pre_h, 0.0)
    eye = lax.broadcasted_iota(jnp.int32, (hid, hid), 0) == lax.broadcasted_iota(jnp.int32, (hid, hid), 1)
    swc = jnp.sum(jnp.where(eye, sw[...], 0.0), axis=1, keepdims=True)
    score = jnp.sum(act * swc, axis=0, keepdims=True)
    weight = jnp.where(is_neg, jnp.exp(adversarial * score), 0.0)
    weighted = jnp.where(is_neg, weight * softplus(score), 0.0)
    positive = jnp.where(is_pos, softplus(-score), 0.0)
    line = jnp.zeros((1, 128), F32)
    for q in range(nq):
        lanes = slice(q * rows, (q + 1) * rows)
        for k, value in enumerate((weight, weighted, positive)):
            total = jnp.sum(value[:, lanes], axis=1, keepdims=True)
            line = jnp.where(lane128 == k * nq + q, total, line)
    tsend[...] = line
    trecv[me] = line

    @pl.loop(1, nodes)
    def _(k):
        pltpu.make_async_remote_copy(
            src_ref=tsend,
            dst_ref=trecv.at[me],
            send_sem=t_send,
            recv_sem=t_recv,
            device_id=node_of((me + k) % nodes),
            device_id_type=MESH,
        ).start()

    pltpu.make_async_copy(trecv.at[pl.ds(0, nodes - 1)], trecv.at[pl.ds(0, nodes - 1)], t_recv).wait()
    totals = jnp.sum(trecv[...], axis=0)
    loss_out[...] = totals[:, 2 * nq : 3 * nq] + totals[:, nq : 2 * nq] / totals[:, :nq]

    total_row = jnp.concatenate(
        [jnp.broadcast_to(totals[:, q : q + 1], (1, rows)) for q in range(nq)], axis=1
    )
    sig = sigmoid(score)
    coef = jnp.where(is_neg, weight / total_row * sig, jnp.where(is_pos, sig - 1.0, 0.0)) / queries_total
    gh = coef * swc * jnp.where(pre_h > 0, 1.0, 0.0)
    gscore = mm(jnp.broadcast_to(coef, (8, nq * rows)), act, NT, HIGH)[0:1]
    ht = jnp.zeros((hid, 128), F32)
    for q in range(nq):
        col = jnp.sum(gh[:, q * rows : (q + 1) * rows], axis=1, keepdims=True)
        ht = jnp.where(lane128 == q, col, ht)
    gqt = mm(mq_w[...], ht, precision=HIGH)
    gquery = mm(qvt, ht, NT, HIGH)
    gent = mm(picked, gh, NT, HIGH)
    gp = mm(me_w[...], gh, precision=HIGH)
    gc = jnp.concatenate(
        [join(mm(split(gp[:, q * rows : (q + 1) * rows], 3), onr[q], NT), 3) for q in range(nq)], axis=1
    )
    gpre = jnp.where(pre > 0, gc, 0.0)
    glayer = mm(s_all, gpre, NT, HIGH)
    gsum = mm(wl[...], gpre, precision=HIGH)
    for q in range(nq):
        col = jnp.sum(gsum[:, q * ent : (q + 1) * ent] * heads[q], axis=1, keepdims=True)
        gqt = gqt + jnp.where(lane128 == q, col, 0.0)
    gs2 = split(jnp.concatenate([gsum[:, q * ent : (q + 1) * ent] for q in range(nq)], axis=0), 2)

    @pl.loop(0, blocks)
    def _(j):
        up = join(mm(gs2, odt[:, cols(j)]), 2) * acc[:, cols(j)]
        et2[:, cols(j)] = split(join(up, nq), 2)

    grel = join(mm(et2[...], ort[...], NT), 2) + join(mm(split(gqt, 3), relhot, NT), 3)

    gmat[...] = jnp.zeros_like(gmat)
    gmat[:, 0:RELP] = grel
    gmat[:, 544 : 544 + dd] = glayer
    gmat[:, 576 : 576 + hid] = gent
    gmat[:, 640 : 640 + hid] = gquery
    gmat[0:1, 704 : 704 + hid] = gscore
    for c in range(6):
        for r in range(4):
            rsrc[c * 4 + r] = gmat[r * 8 : r * 8 + 8, c * 128 : (c + 1) * 128]

    own = me < TILES

    @pl.loop(1, nodes)
    def _(k):
        to = (me + k) % nodes

        @pl.when(to < TILES)
        def _():
            pltpu.make_async_remote_copy(
                src_ref=rsrc.at[to],
                dst_ref=rsbuf.at[me],
                send_sem=r_send,
                recv_sem=r_recv,
                device_id=node_of(to),
                device_id_type=MESH,
            ).start()

    @pl.when(own)
    def _():
        rsbuf[me] = rsrc[me]
        pltpu.make_async_copy(rsbuf.at[pl.ds(0, nodes - 1)], rsbuf.at[pl.ds(0, nodes - 1)], r_recv).wait()
        zbuf[mz] = jnp.sum(rsbuf[...], axis=0)

        @pl.loop(1, zs)
        def _(k):
            pltpu.make_async_remote_copy(
                src_ref=zbuf.at[mz],
                dst_ref=zbuf.at[mz],
                send_sem=z_send,
                recv_sem=z_recv,
                device_id=(me, (mz + k) % zs),
                device_id_type=MESH,
            ).start()

        if zs > 1:
            pltpu.make_async_copy(zbuf.at[pl.ds(0, zs - 1)], zbuf.at[pl.ds(0, zs - 1)], z_recv).wait()
        agbuf[me] = jnp.sum(zbuf[...], axis=0)

        @pl.loop(1, nodes)
        def _(k):
            pltpu.make_async_remote_copy(
                src_ref=agbuf.at[me],
                dst_ref=agbuf.at[me],
                send_sem=a_send,
                recv_sem=a_recv,
                device_id=node_of((me + k) % nodes),
                device_id_type=MESH,
            ).start()

        pltpu.make_async_copy(agbuf.at[pl.ds(0, TILES - 1)], agbuf.at[pl.ds(0, TILES - 1)], a_recv).wait()

    @pl.when(jnp.logical_not(own))
    def _():
        pltpu.make_async_copy(agbuf, agbuf, a_recv).wait()

    for c in range(6):
        for r in range(4):
            gmat[r * 8 : r * 8 + 8, c * 128 : (c + 1) * 128] = agbuf[c * 4 + r]
    for i in range(RELP // 128):
        first, last = i * 128, min(i * 128 + 128, nrel)
        wide = jnp.concatenate([gmat[:, first : first + 128]] * 4, axis=0).T
        grel_out[first:last, :] = wide[: last - first, :dd]
    glayer_out[...] = gmat[:, 544 : 544 + dd]
    gent_out[...] = gmat[:, 576 : 576 + hid]
    gquery_out[...] = gmat[:, 640 : 640 + hid]
    gscore_out[...] = gmat[0:1, 704 : 704 + hid]

    @pl.loop(0, 2 * chips)
    def _(i):
        @pl.when(i != core)
        def _():
            pltpu.make_async_copy(sbuf.at[i], sbuf.at[i], s_send.at[i]).wait()

    pltpu.make_async_copy(trecv.at[pl.ds(0, nodes - 1)], trecv.at[pl.ds(0, nodes - 1)], t_send).wait()

    @pl.when(own)
    def _():
        pltpu.make_async_copy(agbuf.at[pl.ds(0, TILES - 1)], agbuf.at[pl.ds(0, TILES - 1)], r_send).wait()
        if zs > 1:
            pltpu.make_async_copy(zbuf.at[pl.ds(0, zs - 1)], zbuf.at[pl.ds(0, zs - 1)], z_send).wait()
        pltpu.make_async_copy(rsbuf.at[pl.ds(0, nodes - 1)], rsbuf.at[pl.ds(0, nodes - 1)], a_send).wait()

    @pl.when(jnp.logical_not(own))
    def _():
        pltpu.make_async_copy(agbuf, agbuf, r_send).wait()


def body(
    sizes,
    state_in, edge_src, edge_dst, edge_rel, edge_count, send_list, query_head, query_rel, pos_tail,
    neg_ids, rel_table, layer_weight, mlp_entity, mlp_query, score_weight,
):
    nodes, zs, nx, ny = sizes
    ent, width = state_in.shape
    dd = rel_table.shape[1]
    hid = mlp_entity.shape[1]
    nq = width // dd
    nrel = rel_table.shape[0]
    edges = edge_src.shape[0]
    negs = neg_ids.shape[1]
    sds = jax.ShapeDtypeStruct
    vmem = pl.BlockSpec(memory_space=pltpu.VMEM)
    smem = pl.BlockSpec(memory_space=pltpu.SMEM)
    dma = pltpu.SemaphoreType.DMA
    scratch = [
        pltpu.VMEM((3 * width, ent), BF16),
        pltpu.VMEM((nodes, 128), jnp.int32),
        pltpu.VMEM((RELP, 128), F32),
        pltpu.VMEM((3 * dd, RELP), BF16),
        pltpu.VMEM((nodes, 64, 128), F32),
        pltpu.VMEM((nodes, 64, 128), F32),
        pltpu.VMEM((RELP, edges), BF16),
        pltpu.VMEM((ent, edges), BF16),
        pltpu.VMEM((dd, edges), F32),
        pltpu.VMEM((width, edges), F32),
        pltpu.VMEM((3 * width, edges), BF16),
        pltpu.VMEM((2 * dd, edges), BF16),
        pltpu.VMEM((nq, ent, 2 * negs), BF16),
        pltpu.VMEM((1, 128), F32),
        pltpu.VMEM((nodes, 1, 128), F32),
        pltpu.VMEM((dd, 768), F32),
        pltpu.VMEM((TILES, 8, 128), F32),
        pltpu.VMEM((nodes, 8, 128), F32),
        pltpu.VMEM((zs, 8, 128), F32),
        pltpu.VMEM((TILES, 8, 128), F32),
        dma((nodes,)), dma((nodes,)), dma, dma, dma, dma, dma, dma, dma, dma,
    ]
    out = pl.pallas_call(
        functools.partial(kernel, (nodes, zs, nx, ny, nq * zs)),
        out_shape=(
            sds((ent, width), F32),
            sds((1, nq), F32),
            sds((nrel, dd), F32),
            sds((dd, dd), F32),
            sds((dd, hid), F32),
            sds((dd, hid), F32),
            sds((1, hid), F32),
        ),
        in_specs=[vmem] * 11 + [smem] * 4,
        out_specs=[vmem] * 7,
        scratch_shapes=scratch,
        compiler_params=pltpu.CompilerParams(
            collective_id=0, has_side_effects=True, vmem_limit_bytes=48 << 20
        ),
        name="layer",
    )(
        state_in,
        edge_src.reshape(edges // 128, 128),
        edge_dst.reshape(edges // 128, 128),
        edge_rel.reshape(edges // 128, 128),
        send_list.reshape(nodes, 64),
        neg_ids,
        rel_table,
        layer_weight,
        mlp_entity,
        mlp_query,
        score_weight.reshape(1, hid),
        edge_count,
        query_head,
        query_rel,
        pos_tail,
    )
    new_state, loss, grel, glayer, gent, gquery, gscore = out
    return new_state, loss.reshape(nq), grel, glayer, gent, gquery, gscore.reshape(hid)


def solution(mesh):
    nodes, zs = mesh.shape["nodes"], mesh.shape["queries"]
    nx = 4
    ny = nodes // (2 * nx)
    in_specs = (
        P("nodes", "queries"),
        P("nodes"),
        P("nodes"),
        P("nodes"),
        P("nodes"),
        P("nodes", None, None),
        P("queries"),
        P("queries"),
        P("queries"),
        P("queries", "nodes"),
        P(),
        P(),
        P(),
        P(),
        P(),
    )
    out_specs = (P("nodes", "queries"), P("queries"), P(), P(), P(), P(), P())
    return jax.shard_map(
        functools.partial(body, (nodes, zs, nx, ny)),
        mesh=mesh, in_specs=in_specs, out_specs=out_specs, check_vma=False,
    )
```

profile of v0, /device:TPU:1, one launch (start us, length us, event | category | flops | bytes accessed | tf_op | source)
XLA Modules:
  0.0 88.9 jit_solution(17801957642418121598)
XLA Ops:
  1.3 0.0 copy-start
  1.3 0.0 copy-start.1
  1.3 0.0 copy-start.2
  1.3 0.0 copy-start.3
  1.3 0.0 copy-start.4
  1.3 0.0 copy-start.5
  1.3 0.0 copy-start.6
  1.4 0.0 copy-start.7
  1.4 0.0 copy-start.8
  1.4 0.0 copy-start.9
  1.4 0.0 copy-start.10
  1.4 0.0 copy-start.11
  1.4 0.0 copy-start.12
  1.4 1.1 %copy.22.rel = f32[535,32]{1,0:T(8,128)S(1)} copy(f32[535,32]{0,1:T(8,128)} %param.25) | data formatting | bytes 136960 | tf_op args[10]
  2.5 0.0 copy-done
  2.6 0.0 copy-done.1
  2.7 81.9 %layer.1 = (f32[256,128]{1,0:T(8,128)S(1)}, f32[1,4]{1,0:T(1,128)S(1)}, f32[535,32]{1,0:T(8,128)S(1)}, f32[32,32]{1,0:T(8,128)S(1)}, f32[32,64]{1,0:T(8,128)S(1)...) custom-call(f32[256,128]{1,0:T(8,128)S(1)} %copy-done, s32[32,128]{1,0:T(8,128)S(1)} %bitcast.7, s32[32,128]{1,0:T(8,128)S(1)} %bitcast.8, ...), custom_call_target="tpu_custom_call" | custom-call | tf_op jit(solution)/shard_map/layer/pallas_call | solution.py:434
  84.6 0.8 copy.23
  85.4 0.7 copy.31
  86.1 0.5 copy.32
  86.6 0.6 copy.33
  87.2 0.6 copy.34
  87.8 0.6 copy.35
  88.4 0.5 copy.36
  (11 shorter events, 0.0 us)
Async XLA Ops:
  1.3 1.3 %copy-start = (f32[256,128]{1,0:T(8,128)S(1)}, f32[256,128]{1,0:T(8,128)}, u32[]{:S(2)}) copy-start(f32[256,128]{1,0:T(8,128)} %state.1) | copy-start | bytes 393220
  1.3 1.3 %copy-start.1 = (s32[4096]{0:T(1024)S(1)}, s32[4096]{0:T(1024)}, u32[]{:S(2)}) copy-start(s32[4096]{0:T(1024)} %param.16) | copy-start | bytes 49156
  1.3 1.3 %copy-start.2 = (s32[4096]{0:T(1024)S(1)}, s32[4096]{0:T(1024)}, u32[]{:S(2)}) copy-start(s32[4096]{0:T(1024)} %param.17) | copy-start | bytes 49156
  1.3 1.3 %copy-start.3 = (s32[4096]{0:T(1024)S(1)}, s32[4096]{0:T(1024)}, u32[]{:S(2)}) copy-start(s32[4096]{0:T(1024)} %param.18) | copy-start | bytes 49156
  1.3 1.3 %copy-start.4 = (s32[1,32,64]{2,1,0:T(8,128)S(1)}, s32[1,32,64]{2,1,0:T(8,128)}, u32[]{:S(2)}) copy-start(s32[1,32,64]{2,1,0:T(8,128)} %param.20) | copy-start | bytes 24580
  1.3 1.3 %copy-start.5 = (f32[32,32]{1,0:T(8,128)S(1)}, f32[32,32]{1,0:T(8,128)}, u32[]{:S(2)}) copy-start(f32[32,32]{1,0:T(8,128)} %wl.1) | copy-start | bytes 12292
  1.3 1.3 %copy-start.6 = (f32[32,64]{1,0:T(8,128)S(1)}, f32[32,64]{1,0:T(8,128)}, u32[]{:S(2)}) copy-start(f32[32,64]{1,0:T(8,128)} %me_w.1) | copy-start | bytes 24580
  1.4 1.3 %copy-start.7 = (f32[32,64]{1,0:T(8,128)S(1)}, f32[32,64]{1,0:T(8,128)}, u32[]{:S(2)}) copy-start(f32[32,64]{1,0:T(8,128)} %mq_w.1) | copy-start | bytes 24580
  1.4 1.3 %copy-start.8 = (s32[4,128]{1,0:T(4,128)S(1)}, s32[4,128]{1,0:T(4,128)}, u32[]{:S(2)}) copy-start(s32[4,128]{1,0:T(4,128)} %neg.1) | copy-start | bytes 6148
  1.4 1.3 %copy-start.9 = (f32[64]{0:T(128)S(1)}, f32[64]{0:T(128)}, u32[]{:S(2)}) copy-start(f32[64]{0:T(128)} %param.29) | copy-start | bytes 772
  1.4 1.3 %copy-start.10 = (s32[4]{0:T(128)S(1)}, s32[4]{0:T(128)}, u32[]{:S(2)}) copy-start(s32[4]{0:T(128)} %qhead.1) | copy-start | bytes 52
  1.4 1.3 %copy-start.11 = (s32[4]{0:T(128)S(1)}, s32[4]{0:T(128)}, u32[]{:S(2)}) copy-start(s32[4]{0:T(128)} %qrel.1) | copy-start | bytes 52
  1.4 1.3 %copy-start.12 = (s32[4]{0:T(128)S(1)}, s32[4]{0:T(128)}, u32[]{:S(2)}) copy-start(s32[4]{0:T(128)} %ptail.1) | copy-start | bytes 52
where the time goes:
time: 89 us; the launch traced here: 88.9 us
  Pallas kernels  81.9 us (92%)
  local copies, waits for them, and re-layouts  5.45 us (6%)
  between operations  1.51 us (2%)
    pallas_call x1, Pallas kernels, body(): pl.pallas_call(functools.partial(kernel, (nodes, zs, nx, ny, nq * zs)), o...  81.9 us
    unnamed x34, local copies, waits for them, and re-layouts  5.45 us

commit v1 on v0

v1 whole, which is shorter than its diff:
```python
import functools

import jax
import jax.numpy as jnp
from jax import lax
from jax.experimental import pallas as pl
from jax.experimental.pallas import tpu as pltpu
from jax.sharding import PartitionSpec as P

adversarial = 0.5
MESH = pl.DeviceIdType.MESH
HIGH = lax.Precision.HIGHEST
F32 = jnp.float32
BF16 = jnp.bfloat16
NT = (((1,), (1,)), ((), ()))
NN = (((1,), (0,)), ((), ()))
TILES = 24
BLK = 256
WIDE = 512


def mm(a, b, dims=NN, precision=None):
    return lax.dot_general(a, b, dims, precision=precision, preferred_element_type=F32)


def parts_of(x, terms):
    parts = []
    for i in range(terms):
        part = x.astype(BF16)
        parts.append(part)
        if i + 1 < terms:
            x = x - part.astype(F32)
    return parts


def split(x, terms, axis=0):
    return jnp.concatenate(parts_of(x, terms), axis=axis)


def join(y, terms):
    rows = y.shape[0] // terms
    out = y[:rows]
    for i in range(1, terms):
        out = out + y[i * rows : (i + 1) * rows]
    return out


def onehot(row, depth):
    ids = lax.broadcasted_iota(jnp.int32, (depth, row.shape[1]), 0)
    return jnp.where(ids == row, 1.0, 0.0).astype(BF16)


def lanes_of(x, queries, rows):
    return jnp.concatenate([x[q * rows : (q + 1) * rows] for q in range(queries)], axis=1)


def rows_of(x, queries, width):
    return jnp.concatenate([x[:, q * width : (q + 1) * width] for q in range(queries)], axis=0)


def transposed(x):
    r, c = x.shape
    return jnp.concatenate(
        [
            jnp.concatenate([x[i : i + 128, j : j + 128].T for i in range(0, r, 128)], axis=1)
            for j in range(0, c, 128)
        ],
        axis=0,
    )


def softplus(x):
    return jnp.maximum(x, 0.0) + jnp.log1p(jnp.exp(-jnp.abs(x)))


def sigmoid(x):
    return 1.0 / (1.0 + jnp.exp(-x))


def far_first(nx, ny):
    def away(d, n):
        return min(d, n - d)

    steps = [(dx, dy) for dy in range(ny) for dx in range(nx) if (dx, dy) != (0, 0)]
    return sorted(steps, key=lambda s: (-away(s[0], nx) - away(s[1], ny), s))


def kernel(
    cfg,
    h_state, h_esrc, h_edst, h_erel, h_slist, h_neg, h_rel, h_wl, h_me, h_mq, h_sw,
    h_count, h_head, h_qrel, h_tail,
    new_out, loss_out, ag,
    st_v, tab, sbuf, edst, erel, neg, relraw, wl, me_w, mq_w, sw,
    esrc, slist, ecount, qhead, qrel, ptail,
    relpad, rt9, stt_ref, relrow, ort, odt, srcr, srct, msg3, acc, et6,
    tsend, trecv, gmat, rsrc, rsbuf, zbuf,
    i_sem, s_send, s_recv, t_send, t_recv, r_send, r_recv, z_send, z_recv, a_send, a_recv,
):
    nodes, zs, nx, ny, queries_total = cfg
    me = lax.axis_index("nodes")
    mz = lax.axis_index("queries")
    chip = me // 2
    core = me % 2
    cx = chip % nx
    cy = chip // nx
    dd, hid = me_w.shape
    ent = h_state.shape[0]
    nq = h_state.shape[1] // dd
    edges = h_esrc.shape[0]
    bnd = h_slist.shape[1]
    blocks = edges // BLK
    nrel = relraw.shape[1]
    lane128 = lax.broadcasted_iota(jnp.int32, (1, 128), 1)

    def node_of(t):
        return (t, mz)

    loads = [
        pltpu.make_async_copy(src, dst, i_sem.at[i])
        for i, (src, dst) in enumerate(
            (
                (h_slist, slist), (h_state, st_v), (h_state, tab.at[pl.ds(0, ent)]), (h_rel, relraw), (h_erel, erel),
                (h_edst, edst), (h_esrc, esrc), (h_count, ecount), (h_qrel, qrel), (h_head, qhead),
                (h_tail, ptail), (h_neg, neg), (h_wl, wl), (h_me, me_w), (h_mq, mq_w), (h_sw, sw),
            )
        )
    ]
    for load in loads:
        load.start()
    barrier = pltpu.get_barrier_semaphore()

    @pl.loop(1, nodes)
    def _(k):
        pl.semaphore_signal(barrier, inc=1, device_id=node_of((me + k) % nodes), device_id_type=MESH)

    @pl.loop(1, zs)
    def _(k):
        pl.semaphore_signal(barrier, inc=1, device_id=(me, (mz + k) % zs), device_id_type=MESH)

    loads[0].wait()
    loads[1].wait()

    @pl.loop(0, nodes)
    def _(b):
        for k in range(bnd):
            sbuf[pl.ds(b * bnd + k, 1), :] = st_v[pl.ds(slist[b, k], 1), :]

    pl.semaphore_wait(barrier, nodes - 1 + zs - 1)

    def chunk(first, n=1):
        return pl.ds(pl.multiple_of(first * bnd, bnd), n * bnd)

    def send_rows(to):
        pltpu.make_async_remote_copy(
            src_ref=sbuf.at[chunk(to)],
            dst_ref=tab.at[pl.ds(pl.multiple_of(ent + me * bnd, bnd), bnd)],
            send_sem=s_send,
            recv_sem=s_recv,
            device_id=node_of(to),
            device_id_type=MESH,
        ).start()

    for dx, dy in far_first(nx, ny):
        there = 2 * (((cy + dy) % ny) * nx + (cx + dx) % nx)
        send_rows(there + core)
        send_rows(there + 1 - core)
    send_rows(2 * chip + 1 - core)
    tab[pl.ds(pl.multiple_of(ent + me * bnd, bnd), bnd), :] = sbuf[chunk(me), :]

    for load in loads[2:]:
        load.wait()
    stt_ref[...] = transposed(st_v[...])
    relpad[...] = jnp.zeros_like(relpad)
    relpad[:, 0:nrel] = relraw[...]
    rt9[...] = jnp.concatenate([split(relpad[:, h * 256 : (h + 1) * 256], 3) for h in range(3)], axis=0)

    def edge_row(ref, j):
        return jnp.concatenate([ref[pl.ds(2 * j, 1), :], ref[pl.ds(2 * j + 1, 1), :]], axis=1)

    def at_block(j, size=BLK):
        return pl.ds(pl.multiple_of(j * size, size), size)

    def relation(hot, high):
        got = mm(rt9[...], hot)
        out = jnp.zeros((dd, hot.shape[1]), F32)
        for h in range(3):
            out = jnp.where(high == h, join(got[h * 3 * dd : (h + 1) * 3 * dd], 3), out)
        return out

    lane256 = lax.broadcasted_iota(jnp.int32, (1, BLK), 1)

    @pl.loop(0, blocks)
    def _(j):
        row = edge_row(erel, j)
        hot = onehot(row & 255, 256)
        ort[:, at_block(j)] = hot
        relrow[at_block(j), :] = transposed(jnp.concatenate([relation(hot, row >> 8)] * nq, axis=0))
        dst = jnp.where(lane256 + j * BLK < ecount[0], edge_row(edst, j), -1)
        odt[:, at_block(j)] = onehot(dst, ent)

    qr = jnp.full((1, 128), -1, jnp.int32)
    for q in range(nq):
        qr = jnp.where(lane128 == q, qrel[q], qr)
    q_hot = onehot(qr & 255, 256)
    q_high = qr >> 8
    qvt = relation(q_hot, q_high)
    lane_ent = lax.broadcasted_iota(jnp.int32, (1, ent), 1)

    def local_of(g):
        return jnp.where(g // ent == me, g % ent, -1)

    heads = [jnp.where(lane_ent == local_of(qhead[q]), 1.0, 0.0) for q in range(nq)]
    tails = [jnp.where(lane_ent == local_of(ptail[q]), 1.0, 0.0) for q in range(nq)]
    head_term = jnp.concatenate([qvt[:, q : q + 1] * heads[q] for q in range(nq)], axis=1)
    qh = mm(mq_w[...].T, qvt, precision=HIGH)
    qh_wide = jnp.concatenate(
        [jnp.broadcast_to(qh[:, q : q + 1], (hid, 128)) for q in range(nq)] + [qh], axis=1
    )
    eye = lax.broadcasted_iota(jnp.int32, (hid, hid), 0) == lax.broadcasted_iota(jnp.int32, (hid, hid), 1)
    swc = jnp.sum(jnp.where(eye, sw[...], 0.0), axis=1, keepdims=True)
    acc[...] = jnp.zeros_like(acc)

    pltpu.make_async_copy(sbuf.at[chunk(0, nodes - 1)], sbuf.at[chunk(0, nodes - 1)], s_recv).wait()

    def gather(j):
        for u in range(BLK):
            srcr[pl.ds(j * BLK + u, 1), :] = tab[pl.ds(esrc[j * BLK + u], 1), :]
        msg3[at_block(j), :] = split(srcr[at_block(j), :] * relrow[at_block(j), :], 3, axis=1)

    def scatter(j):
        acc[...] += mm(odt[:, at_block(j)], msg3[at_block(j), :])

    gather(0)

    @pl.loop(1, blocks)
    def _(j):
        scatter(j - 1)
        gather(j)

    scatter(blocks - 1)
    width = nq * dd
    summed = acc[:, 0:width] + acc[:, width : 2 * width] + acc[:, 2 * width : 3 * width]
    s_all = lanes_of(transposed(summed), nq, dd) + head_term
    pre = mm(wl[...].T, s_all, precision=HIGH)
    new_all = lanes_of(stt_ref[...], nq, dd) + jnp.maximum(pre, 0.0)

    picks = []
    hots = []
    pos_pick = jnp.zeros((dd, 128), F32)
    is_pos = lane128 < 0
    for q in range(nq):
        mine = new_all[:, q * ent : (q + 1) * ent]
        ids = neg[q : q + 1, :]
        low = jnp.broadcast_to(ids & 127, (dd, 128))
        out = jnp.zeros((dd, 128), F32)
        for b in range(ent // 128):
            got = jnp.take_along_axis(
                mine[:, b * 128 : (b + 1) * 128], low, axis=1, mode="promise_in_bounds"
            )
            out = jnp.where((ids >> 7) == b, got, out)
        picks.append(out)
        hots.append(onehot(ids, ent))
        pos_pick = jnp.where(lane128 == q, jnp.sum(mine * tails[q], axis=1, keepdims=True), pos_pick)
        is_pos = is_pos | ((lane128 == q) & (ptail[q] // ent == me))
    picked = jnp.concatenate(picks + [pos_pick], axis=1)
    pre_h = mm(me_w[...].T, picked, precision=HIGH) + qh_wide
    act = jnp.maximum(pre_h, 0.0)
    score = jnp.sum(act * swc, axis=0, keepdims=True)
    nneg = nq * 128
    s_neg = rows_of(score[:, :nneg], nq, 128)
    s_pos = score[:, nneg:]
    weight = jnp.exp(adversarial * s_neg)
    part_total = jnp.sum(weight, axis=1, keepdims=True)
    part_weighted = jnp.sum(weight * softplus(s_neg), axis=1, keepdims=True)
    sub = lax.broadcasted_iota(jnp.int32, (nq, 128), 0)
    lanes = lax.broadcasted_iota(jnp.int32, (nq, 128), 1)

    def row_of(col, first):
        return jnp.sum(jnp.where(lanes == sub + first, col, 0.0), axis=0, keepdims=True)

    part_row = row_of(part_total, 0)
    pos_terms = jnp.where(is_pos, softplus(-s_pos), 0.0)
    line = part_row + row_of(part_weighted, nq) + pltpu.roll(pos_terms, 2 * nq, 1)
    tsend[...] = line
    trecv[me] = line

    @pl.loop(1, nodes)
    def _(k):
        pltpu.make_async_remote_copy(
            src_ref=tsend,
            dst_ref=trecv.at[me],
            send_sem=t_send,
            recv_sem=t_recv,
            device_id=node_of((me + k) % nodes),
            device_id_type=MESH,
        ).start()

    safe = jnp.where(part_total > 0, part_total, 1.0)
    c_neg = weight / safe * sigmoid(s_neg) / queries_total
    c_pos = jnp.where(is_pos, sigmoid(s_pos) - 1.0, 0.0) / queries_total
    coef = jnp.concatenate([c_neg[q : q + 1] for q in range(nq)] + [c_pos], axis=1)
    gh = coef * swc * jnp.where(pre_h > 0, 1.0, 0.0)
    gp = mm(me_w[...], gh, precision=HIGH)
    gc_neg = jnp.concatenate(
        [join(mm(split(gp[:, q * 128 : (q + 1) * 128], 3), hots[q], NT), 3) for q in range(nq)], axis=1
    )
    gc_pos = jnp.concatenate([gp[:, nneg + q : nneg + q + 1] * tails[q] for q in range(nq)], axis=1)
    gpre = jnp.concatenate([jnp.where(pre > 0, gc_neg, 0.0), jnp.where(pre > 0, gc_pos, 0.0)], axis=1)
    gsum = mm(wl[...], gpre, precision=HIGH)
    half = nq * ent
    gs_neg = rows_of(gsum[:, :half], nq, ent)
    gs_pos = rows_of(gsum[:, half:], nq, ent)

    ht_neg = jnp.zeros((hid, 128), F32)
    hd_neg = jnp.zeros((dd, 128), F32)
    hd_pos = jnp.zeros((dd, 128), F32)
    scores8 = jnp.broadcast_to(coef, (8, nneg + 128))
    ent_q, lay_q, sco_q = [], [], []
    lay_pos = jnp.zeros((dd, dd), F32)
    for q in range(nq):
        tile = slice(q * 128, (q + 1) * 128)
        cols = slice(q * ent, (q + 1) * ent)
        here = lane128 == q
        ht_neg = jnp.where(here, jnp.sum(gh[:, tile], axis=1, keepdims=True), ht_neg)
        hd_neg = jnp.where(here, jnp.sum(gsum[:, cols] * heads[q], axis=1, keepdims=True), hd_neg)
        g_p = gsum[:, half + q * ent : half + (q + 1) * ent]
        hd_pos = jnp.where(here, jnp.sum(g_p * heads[q], axis=1, keepdims=True), hd_pos)
        ent_q.append(mm(picked[:, tile], gh[:, tile], NT, HIGH))
        sco_q.append(mm(scores8[:, tile], act[:, tile], NT, HIGH)[0:1])
        lay_q.append(mm(s_all[:, cols], gpre[:, cols], NT, HIGH))
    lay_pos = mm(s_all, gpre[:, half:], NT, HIGH)
    ent_pos = mm(pos_pick, gh[:, nneg:], NT, HIGH)
    sco_pos = mm(scores8[:, nneg:], act[:, nneg:], NT, HIGH)[0:1]

    @pl.loop(0, edges // BLK)
    def _(j):
        srct[:, at_block(j)] = transposed(srcr[at_block(j), :])

    pltpu.make_async_copy(trecv.at[pl.ds(0, nodes - 1)], trecv.at[pl.ds(0, nodes - 1)], t_recv).wait()
    totals = jnp.sum(trecv[...], axis=0)
    loss_out[...] = pltpu.roll(totals, 128 - 2 * nq, 1) + pltpu.roll(totals, 128 - nq, 1) / totals
    ratio = jnp.where(lane128 < nq, part_row / totals, 0.0)
    ratios = [ratio[:, q : q + 1] for q in range(nq)]
    gs = jnp.concatenate([gs_neg[q * dd : (q + 1) * dd] * ratios[q] for q in range(nq)], axis=0) + gs_pos
    gs2 = split(gs, 2)

    ht = ht_neg * ratio + gh[:, nneg:]
    gq = mm(mq_w[...], ht, precision=HIGH) + hd_neg * ratio + hd_pos
    gquery = mm(qvt, ht, NT, HIGH)
    gent = ent_pos + sum(ent_q[q] * ratios[q] for q in range(nq))
    glayer = lay_pos + sum(lay_q[q] * ratios[q] for q in range(nq))
    gscore = sco_pos + sum(sco_q[q] * ratios[q] for q in range(nq))
    gq9 = split(jnp.concatenate([jnp.where(q_high == h, gq, 0.0) for h in range(3)], axis=0), 3)
    grel_q = join(mm(gq9, q_hot, NT), 3)

    @pl.loop(0, edges // WIDE)
    def _(j):
        c = at_block(j, WIDE)
        up = join(mm(gs2, odt[:, c]), 2) * srct[:, c]
        term = join(up, nq)
        high = jnp.concatenate([erel[pl.ds(4 * j + i, 1), :] for i in range(4)], axis=1) >> 8
        et6[:, c] = split(jnp.concatenate([jnp.where(high == h, term, 0.0) for h in range(3)], axis=0), 2)

    grel = grel_q + join(mm(et6[...], ort[...], NT), 2)

    gmat[...] = jnp.zeros_like(gmat)
    gmat[:, 0:256] = grel[:dd]
    gmat[:, 256:512] = grel[dd : 2 * dd]
    gmat[:, 512:768] = grel[2 * dd :]
    gmat[:, 544 : 544 + dd] = glayer
    gmat[:, 576 : 576 + hid] = gent
    gmat[:, 640 : 640 + hid] = gquery
    gmat[0:1, 704 : 704 + hid] = gscore
    for c in range(6):
        for r in range(4):
            rsrc[c * 4 + r] = gmat[r * 8 : r * 8 + 8, c * 128 : (c + 1) * 128]

    own = me < TILES

    @pl.loop(1, nodes)
    def _(k):
        to = (me + k) % nodes

        @pl.when(to < TILES)
        def _():
            pltpu.make_async_remote_copy(
                src_ref=rsrc.at[to],
                dst_ref=rsbuf.at[me],
                send_sem=r_send,
                recv_sem=r_recv,
                device_id=node_of(to),
                device_id_type=MESH,
            ).start()

    def wait_for(ref, sem):
        pltpu.make_async_copy(ref, ref, sem).wait()

    @pl.when(own)
    def _():
        rsbuf[me] = rsrc[me]
        wait_for(rsbuf.at[pl.ds(0, nodes - 1)], r_recv)
        zbuf[mz] = jnp.sum(rsbuf[...], axis=0)

        @pl.loop(1, zs)
        def _(k):
            pltpu.make_async_remote_copy(
                src_ref=zbuf.at[mz],
                dst_ref=zbuf.at[mz],
                send_sem=z_send,
                recv_sem=z_recv,
                device_id=(me, (mz + k) % zs),
                device_id_type=MESH,
            ).start()

        if zs > 1:
            wait_for(zbuf.at[pl.ds(0, zs - 1)], z_recv)
        ag[me] = jnp.sum(zbuf[...], axis=0)

        @pl.loop(1, nodes)
        def _(k):
            pltpu.make_async_remote_copy(
                src_ref=ag.at[me],
                dst_ref=ag.at[me],
                send_sem=a_send,
                recv_sem=a_recv,
                device_id=node_of((me + k) % nodes),
                device_id_type=MESH,
            ).start()

    new_out[...] = transposed(rows_of(new_all, nq, ent))

    wait_for(sbuf.at[chunk(0, nodes - 1)], s_send)
    wait_for(trecv.at[pl.ds(0, nodes - 1)], t_send)

    @pl.when(own)
    def _():
        wait_for(rsrc.at[pl.ds(0, TILES - 1)], r_send)
        if zs > 1:
            wait_for(zbuf.at[pl.ds(0, zs - 1)], z_send)
        wait_for(ag.at[pl.ds(0, TILES - 1)], a_recv)
        wait_for(rsbuf.at[pl.ds(0, nodes - 1)], a_send)

    @pl.when(jnp.logical_not(own))
    def _():
        wait_for(rsrc, r_send)
        wait_for(ag, a_recv)


def finish(
    new, loss, ag,
    new_o, loss_o, grel_o, glayer_o, gent_o, gquery_o, gscore_o,
    gmat, v_loss, v_rel, v_layer, v_ent, v_query, v_score, sem,
):
    first = pltpu.make_async_copy(new, new_o, sem.at[0])
    first.start()
    for c in range(6):
        for r in range(4):
            gmat[r * 8 : r * 8 + 8, c * 128 : (c + 1) * 128] = ag[c * 4 + r]
    nrel = v_rel.shape[1]
    dd, hid = v_ent.shape
    v_rel[...] = gmat[:, 0:nrel]
    copies = [pltpu.make_async_copy(v_rel, grel_o, sem.at[1])]
    v_layer[...] = gmat[:, 544 : 544 + dd]
    v_ent[...] = gmat[:, 576 : 576 + hid]
    v_query[...] = gmat[:, 640 : 640 + hid]
    v_score[...] = gmat[0:1, 704 : 704 + hid]
    v_loss[...] = loss[:, 0 : v_loss.shape[1]]
    pairs = ((v_layer, glayer_o), (v_ent, gent_o), (v_query, gquery_o), (v_score, gscore_o), (v_loss, loss_o))
    for i, (src, dst) in enumerate(pairs):
        copies.append(pltpu.make_async_copy(src, dst, sem.at[2 + i]))
    for copy in copies:
        copy.start()
    for copy in [first, *copies]:
        copy.wait()


def body(
    sizes,
    state_in, edge_src, edge_dst, edge_rel, edge_count, send_list, query_head, query_rel, pos_tail,
    neg_ids, rel_table, layer_weight, mlp_entity, mlp_query, score_weight,
):
    nodes, zs, nx, ny = sizes
    ent, width = state_in.shape
    nrel, dd = rel_table.shape
    hid = mlp_entity.shape[1]
    nq = width // dd
    edges = edge_src.shape[0]
    bnd = send_list.shape[2]
    sds = jax.ShapeDtypeStruct
    vmem = pl.BlockSpec(memory_space=pltpu.VMEM)
    hbm = pl.BlockSpec(memory_space=pltpu.HBM)
    dma = pltpu.SemaphoreType.DMA
    I32 = jnp.int32
    scratch = [
        pltpu.VMEM((ent, width), F32),
        pltpu.VMEM((ent + nodes * bnd, width), F32),
        pltpu.VMEM((nodes * bnd, width), F32),
        pltpu.VMEM((edges // 128, 128), I32),
        pltpu.VMEM((edges // 128, 128), I32),
        pltpu.VMEM(neg_ids.shape, I32),
        pltpu.VMEM((dd, nrel), F32),
        pltpu.VMEM((dd, dd), F32),
        pltpu.VMEM((dd, hid), F32),
        pltpu.VMEM((dd, hid), F32),
        pltpu.VMEM((1, hid), F32),
        pltpu.SMEM((edges,), I32),
        pltpu.SMEM((nodes, bnd), I32),
        pltpu.SMEM((1,), I32),
        pltpu.SMEM((nq,), I32),
        pltpu.SMEM((nq,), I32),
        pltpu.SMEM((nq,), I32),
        pltpu.VMEM((dd, 768), F32),
        pltpu.VMEM((9 * dd, 256), BF16),
        pltpu.VMEM((width, ent), F32),
        pltpu.VMEM((edges, width), F32),
        pltpu.VMEM((256, edges), BF16),
        pltpu.VMEM((ent, edges), BF16),
        pltpu.VMEM((edges, width), F32),
        pltpu.VMEM((width, edges), F32),
        pltpu.VMEM((edges, 3 * width), BF16),
        pltpu.VMEM((ent, 3 * width), F32),
        pltpu.VMEM((6 * dd, edges), BF16),
        pltpu.VMEM((1, 128), F32),
        pltpu.VMEM((nodes, 1, 128), F32),
        pltpu.VMEM((dd, 768), F32),
        pltpu.VMEM((TILES, 8, 128), F32),
        pltpu.VMEM((nodes, 8, 128), F32),
        pltpu.VMEM((zs, 8, 128), F32),
        dma((16,)), dma, dma, dma, dma, dma, dma, dma, dma, dma, dma,
    ]
    new, loss, ag = pl.pallas_call(
        functools.partial(kernel, (nodes, zs, nx, ny, nq * zs)),
        out_shape=(sds((ent, width), F32), sds((1, 128), F32), sds((TILES, 8, 128), F32)),
        in_specs=[hbm] * 15,
        out_specs=[vmem] * 3,
        scratch_shapes=scratch,
        compiler_params=pltpu.CompilerParams(
            collective_id=0, has_side_effects=True, vmem_limit_bytes=48 << 20
        ),
        name="layer",
    )(
        state_in,
        edge_src,
        edge_dst.reshape(edges // 128, 128),
        edge_rel.reshape(edges // 128, 128),
        send_list.reshape(nodes, bnd),
        neg_ids,
        rel_table.T,
        layer_weight,
        mlp_entity,
        mlp_query,
        score_weight.reshape(1, hid),
        edge_count,
        query_head,
        query_rel,
        pos_tail,
    )
    shapes = [(1, nq), (dd, nrel), (dd, dd), (dd, hid), (dd, hid), (1, hid)]
    new_state, loss, grel, glayer, gent, gquery, gscore = pl.pallas_call(
        finish,
        out_shape=[sds((ent, width), F32)] + [sds(s, F32) for s in shapes],
        in_specs=[vmem] * 3,
        out_specs=[hbm] * 7,
        scratch_shapes=[pltpu.VMEM((dd, 768), F32)] + [pltpu.VMEM(s, F32) for s in shapes] + [dma((7,))],
        name="finish",
    )(new, loss, ag)
    return new_state, loss.reshape(nq), grel.T, glayer, gent, gquery, gscore.reshape(hid)


def solution(mesh):
    nodes, zs = mesh.shape["nodes"], mesh.shape["queries"]
    nx = 4
    ny = nodes // (2 * nx)
    in_specs = (
        P("nodes", "queries"),
        P("nodes"),
        P("nodes"),
        P("nodes"),
        P("nodes"),
        P("nodes", None, None),
        P("queries"),
        P("queries"),
        P("queries"),
        P("queries", "nodes"),
        P(),
        P(),
        P(),
        P(),
        P(),
    )
    out_specs = (P("nodes", "queries"), P("queries"), P(), P(), P(), P(), P())
    return jax.shard_map(
        functools.partial(body, (nodes, zs, nx, ny)),
        mesh=mesh, in_specs=in_specs, out_specs=out_specs, check_vma=False,
    )
```

time: 89 us -> 68.9 us (0.77)
  Pallas kernels: 81.9 us -> 57.5 us
  local copies, waits for them, and re-layouts: 5.45 us -> 9.28 us
    pallas_call x1, Pallas kernels: 81.9 us -> 55.8 us  [body(): pl.pallas_call(functools.partial(kernel, (nodes, zs, nx, ny, nq * zs)), o...]
    unnamed x34, local copies, waits for them, and re-layouts: 5.45 us -> 9.28 us
    pallas_call x0 -> x1, Pallas kernels: none -> 1.71 us  [body(): pl.pallas_call(finish, out_shape=[sds((ent, width), F32)] + [sds(s, F32)...]
where the time goes in v1:
time: 68.9 us; the launch traced here: 68.1 us
  Pallas kernels  57.5 us (83%)
  local copies, waits for them, and re-layouts  9.28 us (13%)
  between operations  1.35 us (2%)
    pallas_call x1, Pallas kernels, body(): pl.pallas_call(functools.partial(kernel, (nodes, zs, nx, ny, nq * zs)), o...  55.8 us
    unnamed x34, local copies, waits for them, and re-layouts  9.28 us
    pallas_call x1, Pallas kernels, body(): pl.pallas_call(finish, out_shape=[sds((ent, width), F32)] + [sds(s, F32)...  1.71 us

profile of v1, /device:TPU:1, one launch (start us, length us, event | category | flops | bytes accessed | tf_op | source)
XLA Modules:
  0.0 68.1 jit_solution(1562022560389490667)
XLA Ops:
  1.3 0.0 copy-start.15
  1.3 0.0 copy-start.11
  1.3 0.0 copy-start.12
  1.3 0.0 copy-start.13
  1.3 0.0 copy-start.14
  1.3 0.6 copy-done.15
  1.9 0.0 copy-done.11
  2.0 0.0 copy-done.12
  2.0 0.0 copy-done.13
  2.0 0.0 copy-done.14
  2.0 0.9 %copy-done.1 = f32[256,128]{1,0:T(8,128)S(1)} copy-done((f32[256,128]{1,0:T(8,128)S(1)}, f32[256,128]{1,0:T(8,128)}, u32[]{:S(2)}) %copy-start.1) | copy-done | bytes 131096
  2.9 0.9 %copy-done.3 = f32[535,32]{0,1:T(8,128)S(1)} copy-done((f32[535,32]{0,1:T(8,128)S(1)}, f32[535,32]{0,1:T(8,128)}, u32[]{:S(2)}) %copy-start.3) | copy-done | bytes 68504
  3.8 0.7 %copy-done.4 = s32[4096]{0:T(1024)S(1)} copy-done((s32[4096]{0:T(1024)S(1)}, s32[4096]{0:T(1024)}, u32[]{:S(2)}) %copy-start.4) | copy-done | bytes 16408
  4.5 0.7 %copy-done.5 = s32[4096]{0:T(1024)S(1)} copy-done((s32[4096]{0:T(1024)S(1)}, s32[4096]{0:T(1024)}, u32[]{:S(2)}) %copy-start.5) | copy-done | bytes 16408
  5.2 0.7 %copy-done.6 = s32[4096]{0:T(1024)S(1)} copy-done((s32[4096]{0:T(1024)S(1)}, s32[4096]{0:T(1024)}, u32[]{:S(2)}) %copy-start.6) | copy-done | bytes 16408
  6.0 0.7 %copy-done.7 = s32[1,32,64]{2,1,0:T(8,128)S(1)} copy-done((s32[1,32,64]{2,1,0:T(8,128)S(1)}, s32[1,32,64]{2,1,0:T(8,128)}, u32[]{:S(2)}) %copy-start.7) | copy-done | bytes 8216
  6.7 0.7 %copy-done.8 = f32[32,32]{1,0:T(8,128)S(1)} copy-done((f32[32,32]{1,0:T(8,128)S(1)}, f32[32,32]{1,0:T(8,128)}, u32[]{:S(2)}) %copy-start.8) | copy-done | bytes 4120
  7.4 0.7 %copy-done.9 = f32[32,64]{1,0:T(8,128)S(1)} copy-done((f32[32,64]{1,0:T(8,128)S(1)}, f32[32,64]{1,0:T(8,128)}, u32[]{:S(2)}) %copy-start.9) | copy-done | bytes 8216
  8.1 0.7 %copy-done.10 = f32[32,64]{1,0:T(8,128)S(1)} copy-done((f32[32,64]{1,0:T(8,128)S(1)}, f32[32,64]{1,0:T(8,128)}, u32[]{:S(2)}) %copy-start.10) | copy-done | bytes 8216
  8.8 55.8 %layer.1 = (f32[256,128]{1,0:T(8,128)S(1)}, f32[1,128]{1,0:T(1,128)S(1)}, f32[24,8,128]{2,1,0:T(8,128)S(1)}) custom-call(f32[256,128]{1,0:T(8,128)S(1)} %copy-done.1, s32[4096]{0:T(1024)S(1)} %copy-done.4, s32[32,128]{1,0:T(8,128)S(1)} %bitcast.9, s32[32,128]{1,0:T(8,128)S(1)} %bitcast.10, s32[32,64]{1,0:T(8,128)S(1)} %bitcast.11, s32[4,128]{1,0:T(4,128)S(1)} %copy-done.11, ...), custom_call_target="tpu_custom_call" | custom-call | tf_op jit(solution)/shard_map/layer/pallas_call | solution.py:531
  64.6 0.7 copy-done
  65.3 0.6 copy-done.2
  65.9 0.5 copy-done.16
  66.4 1.7 %finish.1 = (f32[256,128]{1,0:T(8,128)}, f32[1,4]{1,0:T(1,128)}, f32[32,535]{1,0:T(8,128)}, f32[32,32]{1,0:T(8,128)}, f32[32,64]{1,0:T(8,128)}, /*index=5*/f32[32,64]{1,0:T(8,128)}, f32[1,64]{1,0:T(1,128)}) custom-call(f32[256,128]{1,0:T(8,128)} %copy-done, f32[1,128]{1,0:T(1,128)} %copy-done.16, f32[24,8,128]{2,1,0:T(8,128)} %copy-done.2), custom_call_target="tpu_custom_call" | custom-call | tf_op jit(solution)/shard_map/finish/pallas_call | solution.py:559
  (12 shorter events, 0.0 us)
Async XLA Ops:
  1.3 0.7 copy-start.15
  1.3 0.7 %copy-start.11 = (s32[4,128]{1,0:T(4,128)S(1)}, s32[4,128]{1,0:T(4,128)}, u32[]{:S(2)}) copy-start(s32[4,128]{1,0:T(4,128)} %h_neg.1) | copy-start | bytes 6148
  1.3 0.7 copy-start.12
  1.3 0.7 copy-start.13
  1.3 0.7 copy-start.14
  2.0 0.9 %copy-start.1 = (f32[256,128]{1,0:T(8,128)S(1)}, f32[256,128]{1,0:T(8,128)}, u32[]{:S(2)}) copy-start(f32[256,128]{1,0:T(8,128)} %h_state.1) | copy-start | bytes 393220
  2.9 0.9 %copy-start.3 = (f32[535,32]{0,1:T(8,128)S(1)}, f32[535,32]{0,1:T(8,128)}, u32[]{:S(2)}) copy-start(f32[535,32]{0,1:T(8,128)} %param.25) | copy-start | bytes 205444
  3.8 0.7 %copy-start.4 = (s32[4096]{0:T(1024)S(1)}, s32[4096]{0:T(1024)}, u32[]{:S(2)}) copy-start(s32[4096]{0:T(1024)} %h_esrc.1) | copy-start | bytes 49156
  4.5 0.7 %copy-start.5 = (s32[4096]{0:T(1024)S(1)}, s32[4096]{0:T(1024)}, u32[]{:S(2)}) copy-start(s32[4096]{0:T(1024)} %param.17) | copy-start | bytes 49156
  5.2 0.7 %copy-start.6 = (s32[4096]{0:T(1024)S(1)}, s32[4096]{0:T(1024)}, u32[]{:S(2)}) copy-start(s32[4096]{0:T(1024)} %param.18) | copy-start | bytes 49156
  5.9 0.7 %copy-start.7 = (s32[1,32,64]{2,1,0:T(8,128)S(1)}, s32[1,32,64]{2,1,0:T(8,128)}, u32[]{:S(2)}) copy-start(s32[1,32,64]{2,1,0:T(8,128)} %param.20) | copy-start | bytes 24580
  6.7 0.7 %copy-start.8 = (f32[32,32]{1,0:T(8,128)S(1)}, f32[32,32]{1,0:T(8,128)}, u32[]{:S(2)}) copy-start(f32[32,32]{1,0:T(8,128)} %h_wl.1) | copy-start | bytes 12292
  7.4 0.7 %copy-start.9 = (f32[32,64]{1,0:T(8,128)S(1)}, f32[32,64]{1,0:T(8,128)}, u32[]{:S(2)}) copy-start(f32[32,64]{1,0:T(8,128)} %h_me.1) | copy-start | bytes 24580
  8.1 0.7 %copy-start.10 = (f32[32,64]{1,0:T(8,128)S(1)}, f32[32,64]{1,0:T(8,128)}, u32[]{:S(2)}) copy-start(f32[32,64]{1,0:T(8,128)} %h_mq.1) | copy-start | bytes 24580
  64.6 0.7 copy-start
  65.3 0.6 copy-start.2
  65.9 0.5 copy-start.16

commit v2 on v1

--- a/solution.py
+++ b/solution.py
@@ -535,7 +535,7 @@
         out_specs=[vmem] * 3,
         scratch_shapes=scratch,
         compiler_params=pltpu.CompilerParams(
-            collective_id=0, has_side_effects=True, vmem_limit_bytes=48 << 20
+            collective_id=0, has_side_effects=True
         ),
         name="layer",
     )(

time: 68.9 us -> 59.2 us (0.86)
  local copies, waits for them, and re-layouts: 9.28 us -> 0 us
    unnamed x34 -> x0, local copies, waits for them, and re-layouts: 9.28 us -> none
where the time goes in v2:
time: 59.2 us; the launch traced here: 59.1 us
  Pallas kernels  57.8 us (98%)
  between operations  1.29 us (2%)
    pallas_call x1, Pallas kernels, body(): pl.pallas_call(functools.partial(kernel, (nodes, zs, nx, ny, nq * zs)), o...  56.1 us
    pallas_call x1, Pallas kernels, body(): pl.pallas_call(finish, out_shape=[sds((ent, width), F32)] + [sds(s, F32)...  1.71 us

profile of v2, /device:TPU:1, one launch (start us, length us, event | category | flops | bytes accessed | tf_op | source)
XLA Modules:
  0.0 59.1 jit_solution(16652664615689361169)
XLA Ops:
  1.3 56.1 %layer.1 = (f32[256,128]{1,0:T(8,128)}, f32[1,128]{1,0:T(1,128)}, f32[24,8,128]{2,1,0:T(8,128)}) custom-call(f32[256,128]{1,0:T(8,128)} %h_state.1, s32[4096]{0:T(1024)} %h_esrc.1, s32[32,128]{1,0:T(8,128)} %bitcast.9, s32[32,128]{1,0:T(8,128)} %bitcast.10, s32[32,64]{1,0:T(8,128)} %bitcast.11, s32[4,128]{1,0:T(4,128)} %h_neg.1, f32[32,535]{1,0:T(8,128)} %bitcast.8, ...), custom_call_target="tpu_custom_call" | custom-call | tf_op jit(solution)/shard_map/layer/pallas_call | solution.py:531
  57.4 1.7 %finish.1 = (f32[256,128]{1,0:T(8,128)}, f32[1,4]{1,0:T(1,128)}, f32[32,535]{1,0:T(8,128)}, f32[32,32]{1,0:T(8,128)}, f32[32,64]{1,0:T(8,128)}, /*index=5*/f32[32,64]{1,0:T(8,128)}, f32[1,64]{1,0:T(1,128)}) custom-call(f32[256,128]{1,0:T(8,128)} %get-tuple-element.17.new, f32[1,128]{1,0:T(1,128)} %get-tuple-element.18.loss, f32[24,8,128]{2,1,0:T(8,128)} %get-tuple-element.19.ag), custom_call_target="tpu_custom_call" | custom-call | tf_op jit(solution)/shard_map/finish/pallas_call | solution.py:559

commit v3 on v2

--- a/solution.py
+++ b/solution.py
@@ -140,12 +140,19 @@
     loads[0].wait()
     loads[1].wait()
 
-    @pl.loop(0, nodes)
-    def _(b):
+    for b in range(nodes):
         for k in range(bnd):
-            sbuf[pl.ds(b * bnd + k, 1), :] = st_v[pl.ds(slist[b, k], 1), :]
+            e = b * bnd + k
+            sbuf[e : e + 1, :] = st_v[pl.ds(slist[b, k], 1), :]
 
     pl.semaphore_wait(barrier, nodes - 1 + zs - 1)
+
+    def peers():
+        for dx, dy in far_first(nx, ny):
+            there = 2 * (((cy + dy) % ny) * nx + (cx + dx) % nx)
+            yield there + core
+            yield there + 1 - core
+        yield 2 * chip + 1 - core
 
     def chunk(first, n=1):
         return pl.ds(pl.multiple_of(first * bnd, bnd), n * bnd)
@@ -160,11 +167,8 @@
             device_id_type=MESH,
         ).start()
 
-    for dx, dy in far_first(nx, ny):
-        there = 2 * (((cy + dy) % ny) * nx + (cx + dx) % nx)
-        send_rows(there + core)
-        send_rows(there + 1 - core)
-    send_rows(2 * chip + 1 - core)
+    for to in peers():
+        send_rows(to)
     tab[pl.ds(pl.multiple_of(ent + me * bnd, bnd), bnd), :] = sbuf[chunk(me), :]
 
     for load in loads[2:]:
@@ -178,6 +182,8 @@
         return jnp.concatenate([ref[pl.ds(2 * j, 1), :], ref[pl.ds(2 * j + 1, 1), :]], axis=1)
 
     def at_block(j, size=BLK):
+        if isinstance(j, int):
+            return slice(j * size, (j + 1) * size)
         return pl.ds(pl.multiple_of(j * size, size), size)
 
     def relation(hot, high):
@@ -224,7 +230,8 @@
 
     def gather(j):
         for u in range(BLK):
-            srcr[pl.ds(j * BLK + u, 1), :] = tab[pl.ds(esrc[j * BLK + u], 1), :]
+            e = j * BLK + u
+            srcr[pl.ds(e, 1), :] = tab[pl.ds(esrc[e], 1), :]
         msg3[at_block(j), :] = split(srcr[at_block(j), :] * relrow[at_block(j), :], 3, axis=1)
 
     def scatter(j):
@@ -232,10 +239,11 @@
 
     gather(0)
 
-    @pl.loop(1, blocks)
-    def _(j):
-        scatter(j - 1)
-        gather(j)
+    @pl.loop(0, (blocks - 1) // 5)
+    def _(t):
+        for i in range(5):
+            scatter(5 * t + i)
+            gather(5 * t + i + 1)
 
     scatter(blocks - 1)
     width = nq * dd
@@ -283,15 +291,13 @@
     line = part_row + row_of(part_weighted, nq) + pltpu.roll(pos_terms, 2 * nq, 1)
     tsend[...] = line
     trecv[me] = line
-
-    @pl.loop(1, nodes)
-    def _(k):
+    for to in peers():
         pltpu.make_async_remote_copy(
             src_ref=tsend,
             dst_ref=trecv.at[me],
             send_sem=t_send,
             recv_sem=t_recv,
-            device_id=node_of((me + k) % nodes),
+            device_id=node_of(to),
             device_id_type=MESH,
         ).start()
 
@@ -377,10 +383,7 @@
 
     own = me < TILES
 
-    @pl.loop(1, nodes)
-    def _(k):
-        to = (me + k) % nodes
-
+    def send_tile(to):
         @pl.when(to < TILES)
         def _():
             pltpu.make_async_remote_copy(
@@ -392,6 +395,9 @@
                 device_id_type=MESH,
             ).start()
 
+    for to in peers():
+        send_tile(to)
+
     def wait_for(ref, sem):
         pltpu.make_async_copy(ref, ref, sem).wait()
 
@@ -416,14 +422,13 @@
             wait_for(zbuf.at[pl.ds(0, zs - 1)], z_recv)
         ag[me] = jnp.sum(zbuf[...], axis=0)
 
-        @pl.loop(1, nodes)
-        def _(k):
+        for to in peers():
             pltpu.make_async_remote_copy(
                 src_ref=ag.at[me],
                 dst_ref=ag.at[me],
                 send_sem=a_send,
                 recv_sem=a_recv,
-                device_id=node_of((me + k) % nodes),
+                device_id=node_of(to),
                 device_id_type=MESH,
             ).start()
 

time: 59.2 us -> 56.5 us (0.954)
  Pallas kernels: 57.8 us -> 55 us
    pallas_call x1, Pallas kernels: 56.1 us -> 53.3 us  [body(): pl.pallas_call(functools.partial(kernel, (nodes, zs, nx, ny, nq * zs)), o...]
where the time goes in v3:
time: 56.5 us; the launch traced here: 56.3 us
  Pallas kernels  55 us (97%)
  between operations  1.29 us (2%)
    pallas_call x1, Pallas kernels, body(): pl.pallas_call(functools.partial(kernel, (nodes, zs, nx, ny, nq * zs)), o...  53.3 us
    pallas_call x1, Pallas kernels, body(): pl.pallas_call(finish, out_shape=[sds((ent, width), F32)] + [sds(s, F32)...  1.71 us

profile of v3, /device:TPU:1, one launch (start us, length us, event | category | flops | bytes accessed | tf_op | source)
XLA Modules:
  0.0 56.3 jit_solution(663677113189126934)
XLA Ops:
  1.3 53.3 %layer.1 = (f32[256,128]{1,0:T(8,128)}, f32[1,128]{1,0:T(1,128)}, f32[24,8,128]{2,1,0:T(8,128)}) custom-call(f32[256,128]{1,0:T(8,128)} %h_state.1, s32[4096]{0:T(1024)} %h_esrc.1, s32[32,128]{1,0:T(8,128)} %bitcast.9, s32[32,128]{1,0:T(8,128)} %bitcast.10, s32[32,64]{1,0:T(8,128)} %bitcast.11, s32[4,128]{1,0:T(4,128)} %h_neg.1, f32[32,535]{1,0:T(8,128)} %bitcast.8, ...), custom_call_target="tpu_custom_call" | custom-call | tf_op jit(solution)/shard_map/layer/pallas_call | solution.py:536
  54.6 1.7 %finish.1 = (f32[256,128]{1,0:T(8,128)}, f32[1,4]{1,0:T(1,128)}, f32[32,535]{1,0:T(8,128)}, f32[32,32]{1,0:T(8,128)}, f32[32,64]{1,0:T(8,128)}, /*index=5*/f32[32,64]{1,0:T(8,128)}, f32[1,64]{1,0:T(1,128)}) custom-call(f32[256,128]{1,0:T(8,128)} %get-tuple-element.17.new, f32[1,128]{1,0:T(1,128)} %get-tuple-element.18.loss, f32[24,8,128]{2,1,0:T(8,128)} %get-tuple-element.19.ag), custom_call_target="tpu_custom_call" | custom-call | tf_op jit(solution)/shard_map/finish/pallas_call | solution.py:564

commit v4 on v3

--- a/solution.py
+++ b/solution.py
@@ -16,7 +16,7 @@
 NN = (((1,), (0,)), ((), ()))
 TILES = 24
 BLK = 256
-WIDE = 512
+WIDE = 1024
 
 
 def mm(a, b, dims=NN, precision=None):
@@ -129,30 +129,27 @@
         load.start()
     barrier = pltpu.get_barrier_semaphore()
 
-    @pl.loop(1, nodes)
-    def _(k):
-        pl.semaphore_signal(barrier, inc=1, device_id=node_of((me + k) % nodes), device_id_type=MESH)
-
-    @pl.loop(1, zs)
-    def _(k):
-        pl.semaphore_signal(barrier, inc=1, device_id=(me, (mz + k) % zs), device_id_type=MESH)
-
-    loads[0].wait()
-    loads[1].wait()
-
-    for b in range(nodes):
-        for k in range(bnd):
-            e = b * bnd + k
-            sbuf[e : e + 1, :] = st_v[pl.ds(slist[b, k], 1), :]
-
-    pl.semaphore_wait(barrier, nodes - 1 + zs - 1)
-
     def peers():
         for dx, dy in far_first(nx, ny):
             there = 2 * (((cy + dy) % ny) * nx + (cx + dx) % nx)
             yield there + core
             yield there + 1 - core
         yield 2 * chip + 1 - core
+
+    for to in peers():
+        pl.semaphore_signal(barrier, inc=1, device_id=node_of(to), device_id_type=MESH)
+    for k in range(1, zs):
+        pl.semaphore_signal(barrier, inc=1, device_id=(me, (mz + k) % zs), device_id_type=MESH)
+
+    loads[0].wait()
+    loads[1].wait()
+
+    for b in range(nodes):
+        for k in range(bnd):
+            e = b * bnd + k
+            sbuf[e : e + 1, :] = st_v[pl.ds(slist[b, k], 1), :]
+
+    pl.semaphore_wait(barrier, nodes - 1 + zs - 1)
 
     def chunk(first, n=1):
         return pl.ds(pl.multiple_of(first * bnd, bnd), n * bnd)
@@ -364,7 +361,7 @@
         c = at_block(j, WIDE)
         up = join(mm(gs2, odt[:, c]), 2) * srct[:, c]
         term = join(up, nq)
-        high = jnp.concatenate([erel[pl.ds(4 * j + i, 1), :] for i in range(4)], axis=1) >> 8
+        high = jnp.concatenate([erel[pl.ds(WIDE // 128 * j + i, 1), :] for i in range(WIDE // 128)], axis=1) >> 8
         et6[:, c] = split(jnp.concatenate([jnp.where(high == h, term, 0.0) for h in range(3)], axis=0), 2)
 
     grel = grel_q + join(mm(et6[...], ort[...], NT), 2)

time: 56.5 us -> 55.6 us (0.984)
  Pallas kernels: 55 us -> 54.1 us
    pallas_call x1, Pallas kernels: 53.3 us -> 52.4 us  [body(): pl.pallas_call(functools.partial(kernel, (nodes, zs, nx, ny, nq * zs)), o...]
where the time goes in v4:
time: 55.6 us; the launch traced here: 55.4 us
  Pallas kernels  54.1 us (97%)
  between operations  1.29 us (2%)
    pallas_call x1, Pallas kernels, body(): pl.pallas_call(functools.partial(kernel, (nodes, zs, nx, ny, nq * zs)), o...  52.4 us
    pallas_call x1, Pallas kernels, body(): pl.pallas_call(finish, out_shape=[sds((ent, width), F32)] + [sds(s, F32)...  1.71 us

profile of v4, /device:TPU:1, one launch (start us, length us, event | category | flops | bytes accessed | tf_op | source)
XLA Modules:
  0.0 55.4 jit_solution(17768798861063055411)
XLA Ops:
  1.3 52.4 %layer.1 = (f32[256,128]{1,0:T(8,128)}, f32[1,128]{1,0:T(1,128)}, f32[24,8,128]{2,1,0:T(8,128)}) custom-call(f32[256,128]{1,0:T(8,128)} %h_state.1, s32[4096]{0:T(1024)} %h_esrc.1, s32[32,128]{1,0:T(8,128)} %bitcast.9, s32[32,128]{1,0:T(8,128)} %bitcast.10, s32[32,64]{1,0:T(8,128)} %bitcast.11, s32[4,128]{1,0:T(4,128)} %h_neg.1, f32[32,535]{1,0:T(8,128)} %bitcast.8, ...), custom_call_target="tpu_custom_call" | custom-call | tf_op jit(solution)/shard_map/layer/pallas_call | solution.py:533
  53.7 1.7 %finish.1 = (f32[256,128]{1,0:T(8,128)}, f32[1,4]{1,0:T(1,128)}, f32[32,535]{1,0:T(8,128)}, f32[32,32]{1,0:T(8,128)}, f32[32,64]{1,0:T(8,128)}, /*index=5*/f32[32,64]{1,0:T(8,128)}, f32[1,64]{1,0:T(1,128)}) custom-call(f32[256,128]{1,0:T(8,128)} %get-tuple-element.17.new, f32[1,128]{1,0:T(1,128)} %get-tuple-element.18.loss, f32[24,8,128]{2,1,0:T(8,128)} %get-tuple-element.19.ag), custom_call_target="tpu_custom_call" | custom-call | tf_op jit(solution)/shard_map/finish/pallas_call | solution.py:561
